TPU v7x, 512 devices: a whole 4x4x16 slice. The times are simulated.
512 devices in a mesh: row: 32 (over x, z_hi, core), col: 16 (over z_lo, y).
Axes of the slice: x: 4, y: 4, z: 16 (z_hi: 4, z_lo: 4; z = z_hi * 4 + z_lo), core: 2. Of those that a mesh axis runs over, the one named last changes fastest.
Arguments:
- a_vals: bfloat16 [32, 16, 2, 6, 5, 128, 128], P('row', 'col'), may hold values from -6 to 6
- a_cols: int32 [32, 16, 2, 6, 5], P('row', 'col'), may hold values from 0 to 5, as said below
- b_vals: bfloat16 [32, 16, 6, 8, 128, 128], P('row', 'col'), may hold values from -0.15625 to 0.15625
- b_cols: int32 [32, 16, 6, 8], P('row', 'col'), may hold values from 0 to 11, as said below
- c_cols: int32 [32, 16, 6, 6], P('row', 'col'), may hold values from 0 to 11, as said below
- panel_owner: int32 [32, 32], replicated, may hold values from 0 to 31, as said below
- atom_size: int32 [192], replicated, may hold values from 64 to 128
Outputs:
- product_blocks: bfloat16 [32, 16, 6, 6, 128, 128], P('row', 'col')
Inputs may be any that keep to these rules, and one draw needn't show every extreme that they name: `a_cols`: the 5 indices of one block row are distinct. `b_cols`: the 8 indices of one block row are distinct. `c_cols`: the 6 indices of one block row are distinct. `panel_owner`: each row is a permutation.
All inputs are finite; a program needn't handle non-finite values.
Results may differ from a plain program's by a relative error of at most 0.001.
Values may be sent and summed in bfloat16 or wider, within the bound.
A program may use at most 128 MiB of HBM per device.

v0:
```python
import jax
import jax.numpy as jnp
from jax import lax
from jax.sharding import PartitionSpec as P


def from_root(value, axis, source):
    kept = jnp.where(lax.axis_index(axis) == source, value, 0).astype(value.dtype)
    return lax.psum(kept, axis)


def shifted(block, axis, distance):
    devices = range(lax.axis_size(axis))
    route = [((i - distance) % len(devices), i) for i in devices]
    return lax.ppermute(block, axis, route)


def pick_sizes(indices, table):
    lane_ids = jnp.arange(table.shape[0], dtype=jnp.int32)
    return jnp.sum(jnp.where(indices[..., None] == lane_ids, table, 0), axis=-1)


def panel_term(avals, acols, bvals, bcols, ccols, k_sizes):
    block_size = avals.shape[-1]
    panel_rows = bvals.shape[0]
    inner_sizes = pick_sizes(acols, k_sizes)
    inside = jnp.arange(block_size, dtype=jnp.int32) < inner_sizes[..., None]
    masked = jnp.where(inside[..., None, :], avals, jnp.zeros((), avals.dtype))
    row_ids = jnp.arange(panel_rows, dtype=jnp.int32)
    row_match = acols[:, :, None] == row_ids[None, None, :]
    col_match = bcols[None, :, :, None] == ccols[:, None, None, :]
    selector = (row_match[:, :, :, None, None] & col_match[:, None, :, :, :]).astype(jnp.bfloat16)
    chosen = jnp.einsum(
        "imjns,jnbc->imsbc", selector, bvals, preferred_element_type=jnp.float32
    ).astype(jnp.bfloat16)
    return jnp.einsum("imab,imsbc->isac", masked, chosen, preferred_element_type=jnp.float32)


def local(a_vals, a_cols, b_vals, b_cols, c_cols, panel_owner, atom_size):
    row_id = lax.axis_index("row")
    col_id = lax.axis_index("col")
    row_count = lax.axis_size("row")
    own_a = a_vals[0, 0]
    own_ac = a_cols[0, 0]
    stored_b = b_vals[0, 0]
    stored_bc = b_cols[0, 0]
    targets = c_cols[0, 0]
    panel_rows = own_a.shape[1]
    panel_cols = 2 * panel_rows
    block_size = own_a.shape[-1]

    def panel_sizes(k_panel):
        return lax.dynamic_slice_in_dim(atom_size, k_panel * panel_rows, panel_rows)

    def fetch_panel(fox_step):
        k_panel = (row_id + fox_step) % row_count
        position = panel_owner[row_id, k_panel]
        slot_index = position % 2
        chosen_v = lax.dynamic_index_in_dim(own_a, slot_index, 0, keepdims=False)
        chosen_c = lax.dynamic_index_in_dim(own_ac, slot_index, 0, keepdims=False)
        return (
            from_root(chosen_v, "col", position // 2),
            from_root(chosen_c, "col", position // 2),
        )

    first_v, first_c = fetch_panel(0)
    summed = panel_term(first_v, first_c, stored_b, stored_bc, targets, panel_sizes(row_id))
    moving_v, moving_c = (stored_b, stored_bc)
    fox_step = 1
    moving_v, moving_c = shifted((moving_v, moving_c), "row", -1)
    got_v, got_c = fetch_panel(fox_step)
    k_panel = (row_id + fox_step) % row_count
    summed = summed + panel_term(got_v, got_c, moving_v, moving_c, targets, panel_sizes(k_panel))
    row_sizes = lax.dynamic_slice_in_dim(atom_size, row_id * panel_rows, panel_rows)
    col_table = lax.dynamic_slice_in_dim(atom_size, col_id * panel_cols, panel_cols)
    col_sizes = pick_sizes(targets, col_table)
    lane_ids = jnp.arange(block_size, dtype=jnp.int32)
    inside = (lane_ids[:, None] < row_sizes[:, None, None, None]) & (
        lane_ids[None, :] < col_sizes[:, :, None, None]
    )
    result = jnp.where(inside, summed, jnp.zeros((), summed.dtype)).astype(jnp.bfloat16)
    return result[None, None]


def solution(mesh):
    placed = (
        P("row", "col", None, None, None, None, None),
        P("row", "col", None, None, None),
        P("row", "col", None, None, None, None),
        P("row", "col", None, None),
        P("row", "col", None, None),
        P(),
        P(),
    )
    return jax.shard_map(
        local,
        mesh=mesh,
        in_specs=placed,
        out_specs=P("row", "col", None, None, None, None),
        check_vma=False,
    )
```

profile of v0, /device:TPU:24, one launch (start us, length us, event | category | flops | bytes accessed | tf_op | source)
XLA Modules:
  0.0 249.5 jit_solution(17373059556922149189)
XLA Ops:
  6.5 0.7 copy.40
  7.2 14.4 %collective-permute-start = (s32[6,8]{1,0:T(8,128)S(1)}, s32[6,8]{1,0:T(8,128)S(1)}, u32[]{:S(2)}, u32[]{:S(2)}) collective-permute-start(s32[6,8]{1,0:T(8,128)S(1)} %bitcast.75), channel_id=1, source_target_pairs={{16,0},{32,16},{48,32},{64,48},{80,64},{96,80},{112,96},{128,112},... | collective-permute-start | bytes 584 | tf_op jit(solution)/shard_map/ppermute | solution.py:15
  21.6 2.6 %collective-permute-start.1 = (bf16[6,8,128,128]{3,2,1,0:T(8,128)(2,1)}, bf16[6,8,128,128]{3,2,1,0:T(8,128)(2,1)S(1)}, u32[]{:S(2)}, u32[]{:S(2)}) collective-permute-start(bf16[6,8,128,128]{3,2,1,0:T(8,128)(2,1)} %bitcast.70), channel_id=1, source_target_pairs={{16,0},{32,16},{48,32},{64,48},{80,64},{96,80},{112,96},{128,112},... | collective-permute-start | bytes 4718600 | tf_op jit(solution)/shard_map/ppermute | solution.py:15
  24.2 1.4 fusion.26
  30.5 3.1 %select_bitcast_fusion = (bf16[6,5,128,128]{3,2,1,0:T(8,128)(2,1)}, bf16[6,5,128,128]{3,2,1,0:T(8,128)(2,1)}) fusion(bf16[1,1,2,6,5,128,128]{6,5,4,3,2,1,0:T(8,128)(2,1)} %param.7, s32[]{:T(128)S(6)} %select_n.144, pred[]{:T(512)S(6)} %eq.123, s32[]{:T(128)S(6)} %select_n.131, pred[]{:T(512)S(6)} %eq.115), kind=kLoop, calls=%fused_computation.15 | loop fusion | flops 983040 | bytes 3932170 | tf_op jit(solution)/shard_map/jit(_where)/select_n | solution.py:8
  33.6 0.1 copy.32
  33.8 70.5 %all-reduce = (s32[6,5]{1,0:T(8,128)S(1)}, s32[6,5]{1,0:T(8,128)S(1)}) all-reduce(s32[6,5]{1,0:T(8,128)S(1)} %get-tuple-element.19, s32[6,5]{1,0:T(8,128)S(1)} %get-tuple-element.20), channel_id=1, replica_groups=mesh['row'=32,'col'=16] {'col'}, use_global_device_ids=true, to_apply=%region_4.5 | all-reduce | flops 60 | bytes 480 | tf_op jit(solution)/shard_map/psum | solution.py:9
  104.3 0.1 copy.12
  104.6 0.2 select_reduce_fusion.2
  104.9 0.1 copy.14
  105.0 0.1 copy.16
  105.2 0.3 select_reduce_fusion.1
  105.5 0.1 copy.18
  105.6 0.2 select_reduce_fusion
  106.2 0.1 broadcast_compare_fusion.1
  106.3 5.9 %fusion.5 = bf16[6,5,6,128,128,1]{4,2,5,3,1,0:T(8,128)(2,1)} fusion(bf16[6,8,128,128,1,1]{3,2,1,0,4,5:T(8,128)(2,1)S(1)} %bitcast.71, pred[6,6,8,6]{3,2,1,0:T(8,128)(4,1)S(1)} %get-tuple-element.15, pred[6,5,6]{2,1,0:T(8,128)(4,1)S(1)} %copy.13), kind=kOutput, calls=%fused_computation.9 | convolution fusion | flops 283124160 | bytes 7473012 | tf_op jit(solution)/shard_map/imjns,jnbc->imsbc/dot_general | solution.py:33
  112.2 10.1 %copy.22 = bf16[6,5,6,128,128,1]{3,4,1,2,0,5:T(8,128)(2,1)} copy(bf16[6,5,6,128,128,1]{4,2,5,3,1,0:T(8,128)(2,1)} %fusion.5) | data formatting | bytes 11796480 | tf_op jit(solution)/shard_map/imjns,jnbc->imsbc/dot_general | solution.py:33
  122.2 5.8 %fusion.3 = bf16[6,5,6,128,128,1]{4,2,5,3,1,0:T(8,128)(2,1)} fusion(bf16[6,8,128,128,1,1]{3,2,1,0,4,5:T(8,128)(2,1)S(1)} %bitcast.72, pred[6,6,8,6]{3,2,1,0:T(8,128)(4,1)S(1)} %get-tuple-element.16, pred[6,5,6]{2,1,0:T(8,128)(4,1)S(1)} %copy.17), kind=kOutput, calls=%fused_computation.7 | convolution fusion | flops 283124160 | bytes 7473012 | tf_op jit(solution)/shard_map/imjns,jnbc->imsbc/dot_general | solution.py:33
  128.1 10.1 %copy.27 = bf16[6,5,6,128,128,1]{3,4,1,2,0,5:T(8,128)(2,1)} copy(bf16[6,5,6,128,128,1]{4,2,5,3,1,0:T(8,128)(2,1)} %fusion.3) | data formatting | bytes 11796480 | tf_op jit(solution)/shard_map/imjns,jnbc->imsbc/dot_general | solution.py:33
  138.1 96.2 %all-reduce.4.cloned.1.call-done = (bf16[6,5,128,128]{3,2,1,0:T(8,128)(2,1)}, bf16[6,5,128,128]{3,2,1,0:T(8,128)(2,1)}) async-done(((bf16[6,5,128,128]{3,2,1,0:T(8,128)(2,1)}, bf16[6,5,128,128]{3,2,1,0:T(8,128)(2,1)}), (bf16[6,5,128,128]{3,2,1,0:T(8,128)(2,1)}, bf16[6,5,128,128]{3,2,1,0:T(8,128)(2,1)})) %all-reduce.4.cloned.1.call-update) | async-done | bytes 1966096 | tf_op jit(solution)/shard_map/psum | solution.py:9
  234.3 4.8 %fusion = f32[6,6,128,128,1]{3,2,4,1,0:T(8,128)S(1)} fusion(bf16[6,5,6,128,128,1]{3,4,1,2,0,5:T(8,128)(2,1)} %copy.22, bf16[6,5,128,128]{3,2,1,0:T(8,128)(2,1)} %get-tuple-element.7, pred[6,5,128]{2,1,0:T(8,128)(4,1)S(1)} %iota_compare_fusion.1), kind=kOutput, calls=%fused_computation.2 | convolution fusion | flops 755466240 | bytes 9244416 | tf_op jit(solution)/shard_map/imab,imsbc->isac/dot_general | solution.py:36
  239.1 0.1 copy-done.5
  239.2 2.1 fusion.7
  241.3 1.4 copy.19
  (29 shorter events, 0.8 us)
Async XLA Ops:
  6.5 227.8 %all-reduce.4.cloned.1.call-start = ((), (), s32[]{:S(2)}) async-start(), calls=%async_computation | async-start | bytes 3932160 | tf_op jit(solution)/shard_map/psum | solution.py:9
  7.2 98.9 %collective-permute-start = (s32[6,8]{1,0:T(8,128)S(1)}, s32[6,8]{1,0:T(8,128)S(1)}, u32[]{:S(2)}, u32[]{:S(2)}) collective-permute-start(s32[6,8]{1,0:T(8,128)S(1)} %bitcast.75), channel_id=1, source_target_pairs={{16,0},{32,16},{48,32},{64,48},{80,64},{96,80},{112,96},{128,112},... | collective-permute-start | bytes 584 | tf_op jit(solution)/shard_map/ppermute | solution.py:15
  21.6 100.6 %collective-permute-start.1 = (bf16[6,8,128,128]{3,2,1,0:T(8,128)(2,1)}, bf16[6,8,128,128]{3,2,1,0:T(8,128)(2,1)S(1)}, u32[]{:S(2)}, u32[]{:S(2)}) collective-permute-start(bf16[6,8,128,128]{3,2,1,0:T(8,128)(2,1)} %bitcast.70), channel_id=1, source_target_pairs={{16,0},{32,16},{48,32},{64,48},{80,64},{96,80},{112,96},{128,112},... | collective-permute-start | bytes 4718600 | tf_op jit(solution)/shard_map/ppermute | solution.py:15
  30.5 3.1 %copy-start.2 = (s32[1,1,2,6,5]{3,2,4,1,0:T(2,128)S(1)}, s32[1,1,2,6,5]{3,2,4,1,0:T(2,128)}, u32[]{:S(2)}) copy-start(s32[1,1,2,6,5]{3,2,4,1,0:T(2,128)} %param.8) | copy-start | bytes 724
  30.5 74.1 %copy-start.4 = (s32[192]{0:T(256)S(1)}, s32[192]{0:T(256)}, u32[]{:S(2)}) copy-start(s32[192]{0:T(256)} %param.13) | copy-start | bytes 2308
  30.5 75.0 %copy-start.3 = (s32[1,1,6,6]{3,1,2,0:T(1,128)S(1)}, s32[1,1,6,6]{3,1,2,0:T(1,128)}, u32[]{:S(2)}) copy-start(s32[1,1,6,6]{3,1,2,0:T(1,128)} %param.11) | copy-start | bytes 436
  30.5 75.8 %copy-start.1 = (bf16[1,1,6,8,128,128]{5,4,3,2,1,0:T(8,128)(2,1)S(1)}, bf16[1,1,6,8,128,128]{5,4,3,2,1,0:T(8,128)(2,1)}, u32[]{:S(2)}) copy-start(bf16[1,1,6,8,128,128]{5,4,3,2,1,0:T(8,128)(2,1)} %param.9) | copy-start | bytes 4718596
  234.3 4.8 %copy-start = (bf16[6,5,6,128,128,1]{3,4,1,2,0,5:T(8,128)(2,1)S(1)}, bf16[6,5,6,128,128,1]{3,4,1,2,0,5:T(8,128)(2,1)}, u32[]{:S(2)}) copy-start(bf16[6,5,6,128,128,1]{3,4,1,2,0,5:T(8,128)(2,1)} %copy.27) | copy-start | bytes 17694724
  234.3 4.9 %copy-start.5 = (bf16[6,5,128,128]{3,2,1,0:T(8,128)(2,1)S(1)}, bf16[6,5,128,128]{3,2,1,0:T(8,128)(2,1)}, u32[]{:S(2)}) copy-start(bf16[6,5,128,128]{3,2,1,0:T(8,128)(2,1)} %get-tuple-element.8) | copy-start | bytes 2949124
Sparse Core Ops, SparseCore 0:
  33.7 200.5 all-reduce.3
where the time goes:
time: 254 us; the launch traced here: 250 us
  waiting for transfers between devices  96.2 us (38%)
  blocking collectives  70.5 us (28%)
  local copies, waits for them, and re-layouts  24.5 us (10%)
  matrix products  18.5 us (7%)
  between operations  18.5 us (7%)
  starting transfers between devices  16.9 us (7%)
  other arithmetic  4.39 us (2%)
    psum x1, waiting for transfers between devices, from_root(): return lax.psum(kept, axis)  96.2 us
    psum x1, blocking collectives, from_root(): return lax.psum(kept, axis)  70.5 us
    dot_general x2, local copies, waits for them, and re-layouts, panel_term(): jnp.einsum('imjns,jnbc->imsbc', selector, bvals, preferred_element_type=j...  20.1 us
    ppermute x2, starting transfers between devices, shifted(): return lax.ppermute(block, axis, route)  16.9 us
    dot_general x2, matrix products, panel_term(): jnp.einsum('imjns,jnbc->imsbc', selector, bvals, preferred_element_type=j...  11.7 us
    dot_general x2, matrix products, panel_term(): jnp.einsum('imab,imsbc->isac', masked, chosen, preferred_element_type=jnp...  6.84 us
  transfers between devices with their start and end apart: 3, of which 1 were waited for; matrix products, arithmetic and copies ran while one was open for 15% of the time, Pallas kernels for 0%

commit v1 on v0

v1 whole, which is shorter than its diff:
```python
import functools

import jax
import jax.numpy as jnp
from jax import lax
from jax.experimental import pallas as pl
from jax.experimental.pallas import tpu as pltpu
from jax.sharding import PartitionSpec as P

MESH = pl.DeviceIdType.MESH
BLK = 128
KB = 6
NZA = 5
NZB = 8
NCS = 6
CB = 12
NY = 4
NZ = 4
ROWS = KB * NZA * BLK
SLICE = ROWS // NY
PER = 3
CH = SLICE // PER
HF = CH // 2
NCHUNK = 2 * PER
PIECE = 3
NPIECE = KB * NZB // PIECE


def remote(src, dst, send_sem, recv_sem, device):
    return pltpu.make_async_remote_copy(
        src_ref=src, dst_ref=dst, send_sem=send_sem, recv_sem=recv_sem,
        device_id=device, device_id_type=MESH)


def move_kernel(n_row, n_col, owner_ref, a_ref, ac_ref, b_ref, bc_ref,
                out_ref, acg_ref, bn_ref, bcn_ref,
                sel, r_up, r_dn, r_opp, l_up, l_dn, t_buf, u_in, d_in, u_out, d_out, full,
                s_y1, v_y1, s_z, v_z, s_y2, v_y2, s_b, v_b, s_i, v_i, loc):
    me_r = lax.axis_index("row")
    me_c = lax.axis_index("col")
    y = lax.rem(me_c, NY)
    q = me_c // NY
    y_p = lax.rem(y + 1, NY)
    y_m = lax.rem(y + NY - 1, NY)
    y_o = lax.rem(y + 2, NY)
    dev_p = (me_r, q * NY + y_p)
    dev_m = (me_r, q * NY + y_m)
    dev_u = (me_r, lax.rem(me_c + NY, n_col))
    dev_d = (me_r, lax.rem(me_c + n_col - NY, n_col))
    to_b = (lax.rem(me_r + n_row - 1, n_row), me_c)
    from_b = (lax.rem(me_r + 1, n_row), me_c)

    barrier = pltpu.get_barrier_semaphore()
    for d in range(1, n_col):
        pl.semaphore_signal(barrier, inc=1, device_id=(me_r, lax.rem(me_c + d, n_col)), device_id_type=MESH)
    pl.semaphore_signal(barrier, inc=1, device_id=to_b, device_id_type=MESH)
    pl.semaphore_signal(barrier, inc=1, device_id=from_b, device_id_type=MESH)

    for s in range(2):
        place = owner_ref[me_r, lax.rem(me_r + s, n_row)]
        f0 = (place == 2 * me_c).astype(jnp.float32).astype(jnp.bfloat16)
        f1 = (place == 2 * me_c + 1).astype(jnp.float32).astype(jnp.bfloat16)

        @pl.loop(0, ROWS // HF)
        def _(g):
            at = pl.ds(pl.multiple_of(g * HF, HF), HF)
            sel[s, at, :] = a_ref[0, at, :] * f0 + a_ref[1, at, :] * f1

    pl.semaphore_wait(barrier, n_col + 1)

    own_ac = pltpu.make_async_copy(ac_ref, acg_ref.at[me_c], loc.at[0])
    own_ac.start()
    idx = []
    for d in range(1, n_col):
        cp = remote(ac_ref, acg_ref.at[me_c], s_i.at[d], v_i.at[d], (me_r, lax.rem(me_c + d, n_col)))
        cp.start()
        idx.append(cp)
    cp = remote(bc_ref, bcn_ref, s_i.at[0], v_i.at[0], to_b)
    cp.start()
    idx.append(cp)

    pieces = []

    def piece():
        k = len(pieces)
        if k < NPIECE:
            at = pl.ds(k * PIECE, PIECE)
            cp = remote(b_ref.at[at], bn_ref.at[at], s_b.at[k], v_b.at[k], to_b)
            cp.start()
            pieces.append(cp)

    def rows_of(slice_id, c, off, size):
        return pl.ds(pl.multiple_of(slice_id * SLICE + (c % PER) * CH + off, 16), size)

    def y1(c):
        s = c // PER
        return (
            remote(sel.at[s, rows_of(y_o, c, 0, HF)], l_up.at[c], s_y1.at[c, 0], v_y1.at[c, 0], dev_p),
            remote(sel.at[s, rows_of(y_o, c, HF, HF)], l_dn.at[c], s_y1.at[c, 1], v_y1.at[c, 1], dev_m),
            remote(sel.at[s, rows_of(y_p, c, 0, CH)], r_up.at[c], s_y1.at[c, 2], v_y1.at[c, 2], dev_p),
            remote(sel.at[s, rows_of(y_m, c, 0, CH)], r_dn.at[c], s_y1.at[c, 3], v_y1.at[c, 3], dev_m),
            remote(l_up.at[c], r_opp.at[c, pl.ds(0, HF)], s_y1.at[c, 4], v_y1.at[c, 4], dev_p),
            remote(l_dn.at[c], r_opp.at[c, pl.ds(HF, HF)], s_y1.at[c, 5], v_y1.at[c, 5], dev_m),
        )

    y1s = [y1(c) for c in range(NCHUNK)]

    def first(c):
        for cp in y1s[c][:4]:
            cp.start()

    def relay(c):
        y1s[c][0].wait_recv()
        y1s[c][4].start()
        y1s[c][1].wait_recv()
        y1s[c][5].start()

    def zs(c):
        return (
            remote(u_out.at[c], u_in.at[c], s_z.at[c, 0], v_z.at[c, 0], dev_u),
            remote(d_out.at[c], d_in.at[c], s_z.at[c, 1], v_z.at[c, 1], dev_d),
        )

    zss = [zs(c) for c in range(NCHUNK)]

    def gather_slice(c):
        s = c // PER
        for j in (2, 3, 4, 5):
            y1s[c][j].wait_recv()
        t = sel[s, rows_of(y, c, 0, CH), :] + r_up[c] + r_dn[c] + r_opp[c]
        t_buf[c] = t

        @pl.when(q == 0)
        def _():
            u_out[c] = t
            zss[c][0].start()

        @pl.when(q == NZ - 1)
        def _():
            d_out[c] = t
            zss[c][1].start()

    def y2(c):
        s = c // PER
        own = rows_of(y, c, 0, CH)
        lo = rows_of(y_m, c, 0, HF)
        hi = rows_of(y_p, c, HF, HF)
        return (
            remote(full.at[s, own], full.at[s, own], s_y2.at[c, 0], v_y2.at[c, 0], dev_p),
            remote(full.at[s, own], full.at[s, own], s_y2.at[c, 1], v_y2.at[c, 1], dev_m),
            remote(full.at[s, lo], full.at[s, lo], s_y2.at[c, 2], v_y2.at[c, 2], dev_p),
            remote(full.at[s, hi], full.at[s, hi], s_y2.at[c, 3], v_y2.at[c, 3], dev_m),
        )

    y2s = [y2(c) for c in range(NCHUNK)]

    def chain(c):
        s = c // PER

        @pl.when(q > 0)
        def _():
            zss[c][0].wait_recv()
            u_out[c] = t_buf[c] + u_in[c]

        @pl.when((q > 0) & (q < NZ - 1))
        def _():
            zss[c][0].start()

        @pl.when(q < NZ - 1)
        def _():
            zss[c][1].wait_recv()
            d_out[c] = t_buf[c] + d_in[c]

        @pl.when((q > 0) & (q < NZ - 1))
        def _():
            zss[c][1].start()

        own = rows_of(y, c, 0, CH)

        @pl.when(q < NZ - 1)
        def _():
            full[s, own, :] = u_out[c] + d_in[c]

        @pl.when(q == NZ - 1)
        def _():
            full[s, own, :] = u_out[c]

        y2s[c][0].start()
        y2s[c][1].start()

    def pass_on(c):
        y2s[c][0].wait_recv()
        y2s[c][2].start()
        y2s[c][1].wait_recv()
        y2s[c][3].start()

    first(0)
    first(1)
    piece()
    piece()
    for c in range(NCHUNK + 3):
        if c < NCHUNK:
            relay(c)
        if c + 2 < NCHUNK:
            first(c + 2)
        piece()
        if 0 <= c - 2 < NCHUNK:
            chain(c - 2)
        if 0 <= c - 3 < NCHUNK:
            pass_on(c - 3)
        piece()
        if c < NCHUNK:
            gather_slice(c)
    while len(pieces) < NPIECE:
        piece()
    outs = []
    for s in range(2):
        for c in range(s * PER, (s + 1) * PER):
            y2s[c][2].wait_recv()
            y2s[c][3].wait_recv()
        cp = pltpu.make_async_copy(full.at[s], out_ref.at[s], loc.at[1 + s])
        cp.start()
        outs.append(cp)
    for c in range(NCHUNK):
        for cp in y1s[c]:
            cp.wait_send()
        for cp in y2s[c]:
            cp.wait_send()

        @pl.when(q < NZ - 1)
        def _():
            zss[c][0].wait_send()

        @pl.when(q > 0)
        def _():
            zss[c][1].wait_send()

    own_ac.wait()
    for cp in idx + pieces + outs:
        cp.wait()


def compute_kernel(n_row, owner_ref, size_ref, acg_ref, bc_ref, bcn_ref, cc_ref, a_ref, b_ref, bn_ref, o_ref,
                   table, bbuf, lhs, rhs, sem):
    me_r = lax.axis_index("row")
    me_c = lax.axis_index("col")
    nb = KB * NZB
    loads = []
    for s, ref in enumerate((b_ref, bn_ref)):
        cp = pltpu.make_async_copy(ref, bbuf.at[pl.ds(s * nb, nb)], sem.at[s])
        cp.start()
        loads.append(cp)
    bbuf[2 * nb] = jnp.zeros((BLK, BLK), jnp.bfloat16)
    for s, ref in enumerate((bc_ref, bcn_ref)):
        base = s * KB * CB

        @pl.loop(0, KB * CB)
        def _(e):
            table[base + e] = 2 * nb

        for j in range(KB):
            for n in range(NZB):
                table[base + j * CB + ref[j, n]] = s * nb + j * NZB + n
    roots = []
    for s in range(2):
        place = owner_ref[me_r, lax.rem(me_r + s, n_row)]
        roots.append((place // 2, lax.rem(place, 2), lax.rem(me_r + s, n_row) * KB))
    for cp in loads:
        cp.wait()
    lane = lax.broadcasted_iota(jnp.int32, (BLK, BLK), 1)
    line = lax.broadcasted_iota(jnp.int32, (BLK, BLK), 0)

    @pl.loop(0, KB)
    def _(i):
        for s in range(2):
            holder, slot, first = roots[s]
            for m in range(NZA):
                j = acg_ref[holder, slot, i, m]
                width = size_ref[first + j]
                at = (s * NZA + m) * BLK
                block = a_ref[s, i * NZA + m]
                lhs[:, pl.ds(at, BLK)] = jnp.where(lane < width, block, jnp.zeros((), jnp.bfloat16))
                for t in range(NCS):
                    where = table[s * KB * CB + j * CB + cc_ref[i, t]]
                    rhs[pl.ds(at, BLK), pl.ds(t * BLK, BLK)] = bbuf[where]
        acc = jnp.dot(lhs[...], rhs[...], preferred_element_type=jnp.float32)
        height = size_ref[me_r * KB + i]
        for t in range(NCS):
            wide = size_ref[me_c * CB + cc_ref[i, t]]
            inside = (line < height) & (lane < wide)
            o_ref[i, t] = jnp.where(inside, acc[:, t * BLK:(t + 1) * BLK], 0.0).astype(jnp.bfloat16)


def local(n_row, n_col, a_vals, a_cols, b_vals, b_cols, c_cols, panel_owner, atom_size):
    a = a_vals.reshape(2, ROWS, BLK)
    ac = a_cols.reshape(2, KB, NZA)
    b = b_vals.reshape(KB * NZB, BLK, BLK)
    bc = b_cols.reshape(KB, NZB)
    cc = c_cols.reshape(KB, NCS)
    any_ = pl.BlockSpec(memory_space=pl.ANY)
    vmem = pl.BlockSpec(memory_space=pltpu.VMEM)
    smem = pl.BlockSpec(memory_space=pltpu.SMEM)
    bf = jnp.bfloat16
    dma = pltpu.SemaphoreType.DMA
    panels, acg, bn, bcn = pl.pallas_call(
        functools.partial(move_kernel, n_row, n_col),
        out_shape=(
            jax.ShapeDtypeStruct((2, ROWS, BLK), bf),
            jax.ShapeDtypeStruct((n_col, 2, KB, NZA), jnp.int32),
            jax.ShapeDtypeStruct((KB * NZB, BLK, BLK), bf),
            jax.ShapeDtypeStruct((KB, NZB), jnp.int32),
        ),
        in_specs=[smem, vmem, any_, any_, any_],
        out_specs=(any_, any_, any_, any_),
        scratch_shapes=[
            pltpu.VMEM((2, ROWS, BLK), bf),
            pltpu.VMEM((NCHUNK, CH, BLK), bf),
            pltpu.VMEM((NCHUNK, CH, BLK), bf),
            pltpu.VMEM((NCHUNK, CH, BLK), bf),
            pltpu.VMEM((NCHUNK, HF, BLK), bf),
            pltpu.VMEM((NCHUNK, HF, BLK), bf),
            pltpu.VMEM((NCHUNK, CH, BLK), bf),
            pltpu.VMEM((NCHUNK, CH, BLK), bf),
            pltpu.VMEM((NCHUNK, CH, BLK), bf),
            pltpu.VMEM((NCHUNK, CH, BLK), bf),
            pltpu.VMEM((NCHUNK, CH, BLK), bf),
            pltpu.VMEM((2, ROWS, BLK), bf),
            dma((NCHUNK, 6)), dma((NCHUNK, 6)),
            dma((NCHUNK, 2)), dma((NCHUNK, 2)),
            dma((NCHUNK, 4)), dma((NCHUNK, 4)),
            dma((NPIECE,)), dma((NPIECE,)),
            dma((n_col,)), dma((n_col,)),
            dma((3,)),
        ],
        compiler_params=pltpu.CompilerParams(collective_id=0, has_side_effects=True),
        name="move",
    )(panel_owner, a, ac, b, bc)
    out = pl.pallas_call(
        functools.partial(compute_kernel, n_row),
        out_shape=jax.ShapeDtypeStruct((KB, NCS, BLK, BLK), bf),
        in_specs=[smem, smem, smem, smem, smem, smem, vmem, any_, any_],
        out_specs=vmem,
        scratch_shapes=[
            pltpu.SMEM((2 * KB * CB,), jnp.int32),
            pltpu.VMEM((2 * KB * NZB + 1, BLK, BLK), bf),
            pltpu.VMEM((BLK, 2 * NZA * BLK), bf),
            pltpu.VMEM((2 * NZA * BLK, NCS * BLK), bf),
            dma((2,)),
        ],
        name="product",
    )(panel_owner, atom_size, acg, bc, bcn, cc, panels.reshape(2, KB * NZA, BLK, BLK), b, bn)
    return out.reshape(1, 1, KB, NCS, BLK, BLK)


def solution(mesh):
    placed = (
        P("row", "col", None, None, None, None, None),
        P("row", "col", None, None, None),
        P("row", "col", None, None, None, None),
        P("row", "col", None, None),
        P("row", "col", None, None),
        P(),
        P(),
    )
    return jax.shard_map(
        functools.partial(local, mesh.shape["row"], mesh.shape["col"]),
        mesh=mesh,
        in_specs=placed,
        out_specs=P("row", "col", None, None, None, None),
        check_vma=False,
    )
```

time: 254 us -> 140 us (0.55); the launches traced: 250 us -> 139 us
  Pallas kernels: 0 us -> 135 us
  waiting for transfers between devices: 96.2 us -> 0 us
  blocking collectives: 70.5 us -> 0 us
  local copies, waits for them, and re-layouts: 24.5 us -> 3.92 us
  matrix products: 18.5 us -> 0 us
  between operations: 18.5 us -> 0.01 us
  starting transfers between devices: 16.9 us -> 0 us
  other arithmetic: 4.39 us -> 0 us
    pallas_call x0 -> x2, Pallas kernels: none -> 135 us  [the longest x1 124 us: local(): pl.pallas_call(functools.partial(move_kernel, n_row, n_col), out_shape=(j...]
    psum x1 -> x0, waiting for transfers between devices: 96.2 us -> none  [from_root(): return lax.psum(kept, axis)]
    psum x1 -> x0, blocking collectives: 70.5 us -> none  [from_root(): return lax.psum(kept, axis)]
    dot_general x2 -> x0, local copies, waits for them, and re-layouts: 20.1 us -> none  [panel_term(): jnp.einsum('imjns,jnbc->imsbc', selector, bvals, preferred_element_type=j...]
    dot_general x4 -> x0, matrix products: 18.5 us -> none  [the longest x2 11.7 us: panel_term(): jnp.einsum('imjns,jnbc->imsbc', selector, bvals, preferred_element_type=j...]
    ppermute x2 -> x0, starting transfers between devices: 16.9 us -> none  [shifted(): return lax.ppermute(block, axis, route)]
    select_n x2 -> x0, other arithmetic: 3.07 us -> none  [from_root(): jnp.where(lax.axis_index(axis) == source, value, 0).astype(value.dtype)]
  transfers between devices with their start and end apart: 3 -> 0, of which waited for: 1 -> 0; matrix products, arithmetic and copies ran while one was open for 15% -> 0% of each run, Pallas kernels for 0% -> 0%
where the time goes in v1:
time: 140 us; the launch traced here: 139 us
  Pallas kernels  135 us (96%)
  local copies, waits for them, and re-layouts  3.92 us (3%)
    pallas_call x1, Pallas kernels, local(): pl.pallas_call(functools.partial(move_kernel, n_row, n_col), out_shape=(j...  124 us
    pallas_call x1, Pallas kernels, local(): pl.pallas_call(functools.partial(compute_kernel, n_row), out_shape=jax.Sh...  11.1 us

profile of v1, /device:TPU:24, one launch (start us, length us, event | category | flops | bytes accessed | tf_op | source)
XLA Modules:
  0.0 139.2 jit_solution(10382324281571418379)
XLA Ops:
  0.0 1.3 copy.14
  1.3 1.3 copy.13
  2.6 1.4 copy.8.ac_ref
  3.9 124.2 %move.1 = (bf16[2,3840,128]{2,1,0:T(8,128)(2,1)}, s32[16,2,6,5]{3,2,1,0:T(8,128)}, bf16[48,128,128]{2,1,0:T(8,128)(2,1)}, s32[6,8]{1,0:T(8,128)}) custom-call(s32[32,32]{1,0:T(8,128)} %owner_ref.3, bf16[2,3840,128]{2,1,0:T(8,128)(2,1)} %bitcast.13, s32[2,6,5]{2,1,0:T(8,128)} %copy.8.ac_ref, bf16[48,128,128]{2,1,0:T(8,128)(2,1)} %bitcast.11, s32[6,8]{1,0:T(8,128)} %bitcast.15), custom_call_target="tpu_custom_call" | custom-call | tf_op jit(solution)/shard_map/move/pallas_call | solution.py:305
  128.1 11.1 %product.1 = bf16[6,6,128,128]{3,2,1,0:T(8,128)(2,1)} custom-call(s32[32,32]{1,0:T(8,128)} %owner_ref.3, s32[192]{0:T(256)} %size_ref.1, s32[16,2,6,5]{3,2,1,0:T(8,128)} %get-tuple-element.9.acg_ref, s32[6,8]{1,0:T(8,128)} %bitcast.16, s32[6,8]{1,0:T(8,128)} %get-tuple-element.10.bcn_ref, s32[6,6]{1,0:T(8,128)} %bitcast.17, ...), custom_call_target="tpu_custom_call" | custom-call | tf_op jit(solution)/shard_map/product/pallas_call | solution.py:338

commit v2 on v1

v2 whole, which is shorter than its diff:
```python
import functools

import jax
import jax.numpy as jnp
from jax import lax
from jax.experimental import pallas as pl
from jax.experimental.pallas import tpu as pltpu
from jax.sharding import PartitionSpec as P

MESH = pl.DeviceIdType.MESH
BLK = 128
KB = 6
NZA = 5
NZB = 8
NCS = 6
CB = 12
NY = 4
NZ = 4
ROWS = KB * NZA * BLK
SLICE = ROWS // NY
NH = 4
NB = KB * NZB
PER = 2
CH = SLICE // PER
HF = CH // 2
NCHUNK = 2 * PER
STRIP = 240
PIECE = 1
RB = 12
NRG = 12
B_FIRST = 4
LEGS = 3


def remote(src, dst, send_sem, recv_sem, device):
    return pltpu.make_async_remote_copy(
        src_ref=src, dst_ref=dst, send_sem=send_sem, recv_sem=recv_sem,
        device_id=device, device_id_type=MESH)


def fox_kernel(n_row, n_col, owner_ref, size_ref, bcs_ref, cc_ref, a_ref, ac_ref, b_ref, bc_ref,
               o_ref, acg_ref, bcn_ref,
               a_buf, sel, r_up, r_dn, l_up, l_dn, t_buf, u_in, d_in, u_out, d_out, full0, full1, hold,
               b_own, b_next, part, lhs, rhs, acs, bns,
               s_y1, v_y1, s_z, v_z, s_y2, v_y2, s_b, v_b, s_r, v_r, s_i, v_i, loc):
    full = (full0, full1)
    me_r = lax.axis_index("row")
    me_c = lax.axis_index("col")
    y = lax.rem(me_c, NY)
    q = me_c // NY
    core = lax.rem(me_r, 2)
    chip = me_r // 2
    zh = lax.rem(chip, NH)
    x = chip // NH
    n_x = n_row // (2 * NH)
    y_p = lax.rem(y + 1, NY)
    y_m = lax.rem(y + NY - 1, NY)
    y_o = lax.rem(y + 2, NY)
    dev_p = (me_r, q * NY + y_p)
    dev_m = (me_r, q * NY + y_m)
    dev_u = (me_r, lax.rem(me_c + NY, n_col))
    dev_d = (me_r, lax.rem(me_c + n_col - NY, n_col))
    to_b = (lax.rem(me_r + n_row - 1, n_row), me_c)
    from_b = (lax.rem(me_r + 1, n_row), me_c)

    def odd_at(px, pz):
        return ((px * NH + pz) * 2 + 1, me_c)

    z_next = lax.rem(zh + 1, NH)
    z_last = lax.rem(zh + NH - 1, NH)
    hop = odd_at(x, z_next)
    hop_back = odd_at(x, z_last)
    last = odd_at(lax.rem(x + n_x - (zh == NH - 2).astype(jnp.int32), n_x), z_next)
    last_back = odd_at(lax.rem(x + (zh == NH - 1).astype(jnp.int32), n_x), z_last)

    barrier = pltpu.get_barrier_semaphore()
    for d in range(1, n_col):
        pl.semaphore_signal(barrier, inc=1, device_id=(me_r, lax.rem(me_c + d, n_col)), device_id_type=MESH)
    pl.semaphore_signal(barrier, inc=1, device_id=to_b, device_id_type=MESH)
    pl.semaphore_signal(barrier, inc=1, device_id=from_b, device_id_type=MESH)

    @pl.when(core == 1)
    def _():
        for dev in (hop, hop_back, last, last_back):
            pl.semaphore_signal(barrier, inc=1, device_id=dev, device_id_type=MESH)

    b_load = pltpu.make_async_copy(b_ref, b_own.at[pl.ds(0, NB)], loc.at[1])
    a_loads = []
    for s in range(2):
        cp = pltpu.make_async_copy(a_ref.at[s], a_buf.at[s], loc.at[3 + s])
        cp.start()
        a_loads.append(cp)
    b_load.start()
    for cp in a_loads:
        cp.wait()
    for s in range(2):
        place = owner_ref[me_r, lax.rem(me_r + s, n_row)]
        f0 = (place == 2 * me_c).astype(jnp.float32).astype(jnp.bfloat16)
        f1 = (place == 2 * me_c + 1).astype(jnp.float32).astype(jnp.bfloat16)

        @pl.loop(0, ROWS // STRIP)
        def _(g):
            at = pl.ds(pl.multiple_of(g * STRIP, STRIP), STRIP)
            sel[s, at, :] = a_buf[0, at, :] * f0 + a_buf[1, at, :] * f1

    pl.semaphore_wait(barrier, n_col + 1 + 4 * core)

    straight = [remote(b_ref.at[pl.ds(k * PIECE, PIECE)], b_next.at[pl.ds(k * PIECE, PIECE)],
                       s_b.at[k], v_b.at[k], to_b) for k in range(NB // PIECE)]
    n_even = (NB - RB) // PIECE
    RG = RB // NRG

    def round_copies(g):
        at = pl.ds(NB - RB + g * RG, RG)
        return (
            remote(b_ref.at[at], hold.at[0, g], s_r.at[g, 0], v_r.at[g, 0], from_b),
            remote(hold.at[0, g], hold.at[1, g], s_r.at[g, 1], v_r.at[g, 1], hop),
            remote(hold.at[1, g], hold.at[2, g], s_r.at[g, 2], v_r.at[g, 2], hop),
            remote(hold.at[2, g], b_next.at[at], s_r.at[g, 3], v_r.at[g, 3], last),
        )

    rounds = [round_copies(g) for g in range(NRG)]
    done = [0, 0]
    legs = [(0, g, k) for k in range(3) for g in range(len(rounds))]

    def more_b(count):
        lo, hi = done[0], min(n_even, done[0] + count)
        done[0] = hi

        @pl.when(core == 0)
        def _():
            for k in range(lo, hi):
                straight[k].start()

    def leg(count):
        lo, hi = done[1], min(len(legs), done[1] + count)
        done[1] = hi

        @pl.when(core == 1)
        def _():
            for _t, g, k in legs[lo:hi]:
                rounds[g][k].wait_recv()
                rounds[g][k + 1].start()

    own_ac = pltpu.make_async_copy(ac_ref, acg_ref.at[me_c], loc.at[0])
    own_ac.start()

    @pl.when(core == 0)
    def _():
        for cps in rounds:
            cps[0].start()

    @pl.when(core == 1)
    def _():
        for cp in straight:
            cp.start()

    idx = []
    for d in range(1, n_col):
        cp = remote(ac_ref, acg_ref.at[me_c], s_i.at[d], v_i.at[d], (me_r, lax.rem(me_c + d, n_col)))
        cp.start()
        idx.append(cp)
    cp = remote(bc_ref, bcn_ref, s_i.at[0], v_i.at[0], to_b)
    cp.start()
    idx.append(cp)

    def rows_of(slice_id, c, off, size):
        return pl.ds(pl.multiple_of(slice_id * SLICE + (c % PER) * CH + off, 16), size)

    def y1(c):
        s = c // PER
        return (
            remote(sel.at[s, rows_of(y_o, c, 0, HF)], l_up.at[c], s_y1.at[c, 0], v_y1.at[c, 0], dev_p),
            remote(sel.at[s, rows_of(y_o, c, HF, HF)], l_dn.at[c], s_y1.at[c, 1], v_y1.at[c, 1], dev_m),
            remote(sel.at[s, rows_of(y_p, c, 0, CH)], r_up.at[c], s_y1.at[c, 2], v_y1.at[c, 2], dev_p),
            remote(sel.at[s, rows_of(y_m, c, 0, CH)], r_dn.at[c], s_y1.at[c, 3], v_y1.at[c, 3], dev_m),
        )

    def zs(c):
        return (
            remote(u_out.at[c], u_in.at[c], s_z.at[c, 0], v_z.at[c, 0], dev_u),
            remote(d_out.at[c], d_in.at[c], s_z.at[c, 1], v_z.at[c, 1], dev_d),
        )

    def y2(c):
        s = c // PER
        own = rows_of(y, c, 0, CH)
        lo = rows_of(y_m, c, 0, HF)
        hi = rows_of(y_p, c, HF, HF)
        return (
            remote(full[s].at[own], full[s].at[own], s_y2.at[c, 0], v_y2.at[c, 0], dev_p),
            remote(full[s].at[own], full[s].at[own], s_y2.at[c, 1], v_y2.at[c, 1], dev_m),
            remote(full[s].at[lo], full[s].at[lo], s_y2.at[c, 2], v_y2.at[c, 2], dev_p),
            remote(full[s].at[hi], full[s].at[hi], s_y2.at[c, 3], v_y2.at[c, 3], dev_m),
        )

    y1s = [y1(c) for c in range(NCHUNK)]
    zss = [zs(c) for c in range(NCHUNK)]
    y2s = [y2(c) for c in range(NCHUNK)]

    def first(c):
        y1s[c][0].start()
        y1s[c][1].start()

    def relay(c):
        s = c // PER
        y1s[c][0].wait_recv()
        at = rows_of(y_p, c, 0, HF)
        sel[s, at, :] = sel[s, at, :] + l_up[c]
        y1s[c][1].wait_recv()
        at = rows_of(y_m, c, HF, HF)
        sel[s, at, :] = sel[s, at, :] + l_dn[c]
        y1s[c][2].start()
        y1s[c][3].start()

    def up(c):
        zss[c][0].wait_recv()
        u_out[c] = t_buf[c] + u_in[c]
        zss[c][0].start()

    def down(c):
        zss[c][1].wait_recv()
        d_out[c] = t_buf[c] + d_in[c]
        zss[c][1].start()

    def gather_slice(c):
        for j in (2, 3):
            y1s[c][j].wait_recv()
        t = sel[c // PER, rows_of(y, c, 0, CH), :] + r_up[c] + r_dn[c]
        t_buf[c] = t

        @pl.when(q == 0)
        def _():
            u_out[c] = t
            zss[c][0].start()

        @pl.when(q == NZ - 1)
        def _():
            d_out[c] = t
            zss[c][1].start()

    def spread(c, value):
        full[c // PER][rows_of(y, c, 0, CH), :] = value
        y2s[c][0].start()
        y2s[c][1].start()

    def chain_a(c):
        @pl.when(q == 1)
        def _():
            up(c)

        @pl.when(q == 2)
        def _():
            down(c)

    def chain_b(c):
        @pl.when(q == 2)
        def _():
            up(c)
            spread(c, u_out[c] + d_in[c])

        @pl.when(q == 1)
        def _():
            down(c)
            spread(c, u_out[c] + d_in[c])

    def chain_c(c):
        @pl.when(q == 0)
        def _():
            zss[c][1].wait_recv()
            spread(c, t_buf[c] + d_in[c])

        @pl.when(q == NZ - 1)
        def _():
            zss[c][0].wait_recv()
            spread(c, t_buf[c] + u_in[c])

    def pass_on(c):
        y2s[c][0].wait_recv()
        y2s[c][2].start()
        y2s[c][1].wait_recv()
        y2s[c][3].start()

    lane = lax.broadcasted_iota(jnp.int32, (BLK, BLK), 1)
    line = lax.broadcasted_iota(jnp.int32, (BLK, BLK), 0)
    b_own[NB] = jnp.zeros((BLK, BLK), jnp.bfloat16)
    b_next[NB] = jnp.zeros((BLK, BLK), jnp.bfloat16)

    def multiply(s, lo, hi):
        k_panel = lax.rem(me_r + s, n_row)
        place = owner_ref[me_r, k_panel]
        holder = place // 2
        slot = lax.rem(place, 2)
        blocks = (b_own, b_next)[s]
        cols = (bcs_ref, bns)[s]

        @pl.loop(lo, hi)
        def _(i):
            targets = [cc_ref[i, 0, t] for t in range(NCS)]
            for m in range(NZA):
                j = acs[holder, m, slot, i]
                width = size_ref[k_panel * KB + j]
                block = full[s][pl.ds(pl.multiple_of((i * NZA + m) * BLK, BLK), BLK), :]
                lhs[:, m * BLK:(m + 1) * BLK] = jnp.where(lane < width, block, jnp.zeros((), jnp.bfloat16))
                found = [cols[j, 0, n] for n in range(NZB)]
                for t in range(NCS):
                    where = jnp.int32(NB)
                    for n in range(NZB):
                        where = jnp.where(found[n] == targets[t], j * NZB + n, where)
                    rhs[m * BLK:(m + 1) * BLK, t * BLK:(t + 1) * BLK] = blocks[where]
            acc = jnp.dot(lhs[...], rhs[...], preferred_element_type=jnp.float32)
            if s == 0:
                part[i] = acc
            else:
                acc = acc + part[i]
                height = size_ref[me_r * KB + i]
                for t in range(NCS):
                    wide = size_ref[me_c * CB + targets[t]]
                    inside = (line < height) & (lane < wide)
                    o_ref[i, t] = jnp.where(inside, acc[:, t * BLK:(t + 1) * BLK], 0.0).astype(jnp.bfloat16)

    def indices():
        own_ac.wait()
        for cp in idx:
            cp.wait()
        pair = [pltpu.make_async_copy(acg_ref, acs, loc.at[2]), pltpu.make_async_copy(bcn_ref, bns, loc.at[0])]
        for cp in pair:
            cp.start()
        for cp in pair:
            cp.wait()
        b_load.wait()

    def landed(s):
        for c in range(s * PER, (s + 1) * PER):
            y2s[c][2].wait_recv()
            y2s[c][3].wait_recv()

    first(0)
    first(1)
    steps = NCHUNK + 5
    more_b(B_FIRST)
    leg(LEGS)
    per = -(-(n_even - B_FIRST) // (steps - 1))
    for c in range(steps):
        for lag, act in ((5, pass_on), (4, chain_c), (3, chain_b), (2, chain_a), (1, gather_slice), (0, relay)):
            if 0 <= c - lag < NCHUNK:
                act(c - lag)
        if c + 2 < NCHUNK:
            first(c + 2)
        more_b(per)
        leg(LEGS)
        if c == steps - 6:
            indices()
    more_b(NB)
    landed(0)
    leg(LEGS * 2)
    multiply(0, 0, KB)
    leg(len(legs))
    landed(1)
    for c in range(NCHUNK):
        for cp in y1s[c]:
            cp.wait_send()
        for cp in y2s[c]:
            cp.wait_send()

        @pl.when(q < NZ - 1)
        def _():
            zss[c][0].wait_send()

        @pl.when(q > 0)
        def _():
            zss[c][1].wait_send()

    @pl.when(core == 0)
    def _():
        for cp in straight[:n_even]:
            cp.wait_send()
        for cps in rounds:
            cps[0].wait_send()
        for cp in straight:
            cp.wait_recv()

    @pl.when(core == 1)
    def _():
        for cp in straight[:n_even]:
            cp.wait_recv()
        for cps in rounds:
            cps[3].wait_recv()
            for cp in cps[1:]:
                cp.wait_send()
        for cp in straight:
            cp.wait_send()

    multiply(1, 0, KB)


def local(n_row, n_col, a_vals, a_cols, b_vals, b_cols, c_cols, panel_owner, atom_size):
    a = a_vals.reshape(2, ROWS, BLK)
    ac = jnp.transpose(a_cols[0, 0], (2, 0, 1))
    b = b_vals.reshape(KB * NZB, BLK, BLK)
    bc = b_cols.reshape(KB, 1, NZB)
    cc = c_cols.reshape(KB, 1, NCS)
    any_ = pl.BlockSpec(memory_space=pl.ANY)
    vmem = pl.BlockSpec(memory_space=pltpu.VMEM)
    smem = pl.BlockSpec(memory_space=pltpu.SMEM)
    bf = jnp.bfloat16
    dma = pltpu.SemaphoreType.DMA
    out, _, _ = pl.pallas_call(
        functools.partial(fox_kernel, n_row, n_col),
        out_shape=(
            jax.ShapeDtypeStruct((KB, NCS, BLK, BLK), bf),
            jax.ShapeDtypeStruct((n_col, NZA, 2, KB), jnp.int32),
            jax.ShapeDtypeStruct((KB, 1, NZB), jnp.int32),
        ),
        in_specs=[smem, smem, smem, smem, any_, any_, any_, any_],
        out_specs=(vmem, any_, any_),
        scratch_shapes=[
            pltpu.VMEM((2, ROWS, BLK), bf),
            pltpu.VMEM((2, ROWS, BLK), bf),
            pltpu.VMEM((NCHUNK, CH, BLK), bf),
            pltpu.VMEM((NCHUNK, CH, BLK), bf),
            pltpu.VMEM((NCHUNK, HF, BLK), bf),
            pltpu.VMEM((NCHUNK, HF, BLK), bf),
            pltpu.VMEM((NCHUNK, CH, BLK), bf),
            pltpu.VMEM((NCHUNK, CH, BLK), bf),
            pltpu.VMEM((NCHUNK, CH, BLK), bf),
            pltpu.VMEM((NCHUNK, CH, BLK), bf),
            pltpu.VMEM((NCHUNK, CH, BLK), bf),
            pltpu.VMEM((ROWS, BLK), bf),
            pltpu.VMEM((ROWS, BLK), bf),
            pltpu.VMEM((3, NRG, RB // NRG, BLK, BLK), bf),
            pltpu.VMEM((NB + 1, BLK, BLK), bf),
            pltpu.VMEM((NB + 1, BLK, BLK), bf),
            pltpu.VMEM((KB, BLK, NCS * BLK), jnp.float32),
            pltpu.VMEM((BLK, NZA * BLK), bf),
            pltpu.VMEM((NZA * BLK, NCS * BLK), bf),
            pltpu.SMEM((n_col, NZA, 2, KB), jnp.int32),
            pltpu.SMEM((KB, 1, NZB), jnp.int32),
            dma((NCHUNK, 4)), dma((NCHUNK, 4)),
            dma((NCHUNK, 2)), dma((NCHUNK, 2)),
            dma((NCHUNK, 4)), dma((NCHUNK, 4)),
            dma((NB // PIECE,)), dma((NB // PIECE,)),
            dma((NRG, 4)), dma((NRG, 4)),
            dma((n_col,)), dma((n_col,)),
            dma((5,)),
        ],
        compiler_params=pltpu.CompilerParams(collective_id=0, has_side_effects=True),
        name="fox",
    )(panel_owner, atom_size, bc, cc, a, ac, b, bc)
    return out.reshape(1, 1, KB, NCS, BLK, BLK)


def solution(mesh):
    placed = (
        P("row", "col", None, None, None, None, None),
        P("row", "col", None, None, None),
        P("row", "col", None, None, None, None),
        P("row", "col", None, None),
        P("row", "col", None, None),
        P(),
        P(),
    )
    return jax.shard_map(
        functools.partial(local, mesh.shape["row"], mesh.shape["col"]),
        mesh=mesh,
        in_specs=placed,
        out_specs=P("row", "col", None, None, None, None),
        check_vma=False,
    )
```

time: 140 us -> 108 us (0.77)
  the two profiles are of different devices: /device:TPU:24 before, /device:TPU:13 now
where the time goes in v2:
time: 108 us
  Pallas kernels  105 us (97%)
  local copies, waits for them, and re-layouts  2.41 us (2%)
    pallas_call x1, Pallas kernels, local(): pl.pallas_call(functools.partial(fox_kernel, n_row, n_col), out_shape=(ja...  105 us
    unnamed x1, local copies, waits for them, and re-layouts  2.41 us

profile of v2, /device:TPU:13, one launch (start us, length us, event | category | flops | bytes accessed | tf_op | source)
XLA Modules:
  0.0 107.8 jit_solution(179153920161491561)
XLA Ops:
  0.0 105.4 %fox.1 = (bf16[6,6,128,128]{3,2,1,0:T(8,128)(2,1)}, s32[16,5,2,6]{3,2,1,0:T(2,128)}, s32[6,1,8]{2,1,0:T(1,128)}) custom-call(s32[32,32]{1,0:T(8,128)} %owner_ref.1, s32[192]{0:T(256)} %size_ref.1, s32[6,1,8]{2,1,0:T(1,128)} %bitcast.11, s32[6,1,6]{2,1,0:T(1,128)} %bitcast.14, bf16[2,3840,128]{2,1,0:T(8,128)(2,1)} %bitcast.8, s32[5,2,6]{2,1,0:T(2,128)} %bitcast.13, ...), custom_call_target="tpu_custom_call" | custom-call | tf_op jit(solution)/shard_map/fox/pallas_call | solution.py:408
  105.4 2.4 %copy.9 = bf16[1,1,6,6,128,128]{5,4,3,2,1,0:T(8,128)(2,1)} copy(bf16[1,1,6,6,128,128]{5,4,3,2,1,0:T(8,128)(2,1)} %bitcast.10) | data formatting | bytes 2359296

commit v3 on v2

--- a/solution.py
+++ b/solution.py
@@ -25,11 +25,13 @@
 HF = CH // 2
 NCHUNK = 2 * PER
 STRIP = 240
-PIECE = 1
-RB = 12
-NRG = 12
-B_FIRST = 4
-LEGS = 3
+RB = 8
+NPB = 2 * NZB
+FRONT = 8
+MID = 3
+L_FRONT = 8
+L_MID = 2
+L_LATE = 8
 
 
 def remote(src, dst, send_sem, recv_sem, device):
@@ -41,9 +43,10 @@
 def fox_kernel(n_row, n_col, owner_ref, size_ref, bcs_ref, cc_ref, a_ref, ac_ref, b_ref, bc_ref,
                o_ref, acg_ref, bcn_ref,
                a_buf, sel, r_up, r_dn, l_up, l_dn, t_buf, u_in, d_in, u_out, d_out, full0, full1, hold,
-               b_own, b_next, part, lhs, rhs, acs, bns,
+               b_own, b_n0, b_n1, b_n2, part, lhs, rhs, lhs2, rhs2, acs, bns,
                s_y1, v_y1, s_z, v_z, s_y2, v_y2, s_b, v_b, s_r, v_r, s_i, v_i, loc):
     full = (full0, full1)
+    b_next = (b_n0, b_n1, b_n2)
     me_r = lax.axis_index("row")
     me_c = lax.axis_index("col")
     y = lax.rem(me_c, NY)
@@ -105,21 +108,20 @@
 
     pl.semaphore_wait(barrier, n_col + 1 + 4 * core)
 
-    straight = [remote(b_ref.at[pl.ds(k * PIECE, PIECE)], b_next.at[pl.ds(k * PIECE, PIECE)],
-                       s_b.at[k], v_b.at[k], to_b) for k in range(NB // PIECE)]
-    n_even = (NB - RB) // PIECE
-    RG = RB // NRG
+    straight = [remote(b_ref.at[k], b_next[k // NPB].at[k % NPB],
+                       s_b.at[k], v_b.at[k], to_b) for k in range(NB)]
+    n_even = NB - RB
 
     def round_copies(g):
-        at = pl.ds(NB - RB + g * RG, RG)
+        k = NB - RB + g
         return (
-            remote(b_ref.at[at], hold.at[0, g], s_r.at[g, 0], v_r.at[g, 0], from_b),
+            remote(b_ref.at[k], hold.at[0, g], s_r.at[g, 0], v_r.at[g, 0], from_b),
             remote(hold.at[0, g], hold.at[1, g], s_r.at[g, 1], v_r.at[g, 1], hop),
             remote(hold.at[1, g], hold.at[2, g], s_r.at[g, 2], v_r.at[g, 2], hop),
-            remote(hold.at[2, g], b_next.at[at], s_r.at[g, 3], v_r.at[g, 3], last),
+            remote(hold.at[2, g], b_next[k // NPB].at[k % NPB], s_r.at[g, 3], v_r.at[g, 3], last),
         )
 
-    rounds = [round_copies(g) for g in range(NRG)]
+    rounds = [round_copies(g) for g in range(RB)]
     done = [0, 0]
     legs = [(0, g, k) for k in range(3) for g in range(len(rounds))]
 
@@ -284,40 +286,78 @@
     lane = lax.broadcasted_iota(jnp.int32, (BLK, BLK), 1)
     line = lax.broadcasted_iota(jnp.int32, (BLK, BLK), 0)
     b_own[NB] = jnp.zeros((BLK, BLK), jnp.bfloat16)
-    b_next[NB] = jnp.zeros((BLK, BLK), jnp.bfloat16)
-
-    def multiply(s, lo, hi):
-        k_panel = lax.rem(me_r + s, n_row)
-        place = owner_ref[me_r, k_panel]
+    for ref in b_next:
+        ref[NPB] = jnp.zeros((BLK, BLK), jnp.bfloat16)
+
+    def multiply_first():
+        place = owner_ref[me_r, me_r]
         holder = place // 2
         slot = lax.rem(place, 2)
-        blocks = (b_own, b_next)[s]
-        cols = (bcs_ref, bns)[s]
-
-        @pl.loop(lo, hi)
+
+        @pl.loop(0, KB)
         def _(i):
             targets = [cc_ref[i, 0, t] for t in range(NCS)]
             for m in range(NZA):
                 j = acs[holder, m, slot, i]
-                width = size_ref[k_panel * KB + j]
-                block = full[s][pl.ds(pl.multiple_of((i * NZA + m) * BLK, BLK), BLK), :]
+                width = size_ref[me_r * KB + j]
+                block = full0[pl.ds(pl.multiple_of((i * NZA + m) * BLK, BLK), BLK), :]
                 lhs[:, m * BLK:(m + 1) * BLK] = jnp.where(lane < width, block, jnp.zeros((), jnp.bfloat16))
-                found = [cols[j, 0, n] for n in range(NZB)]
+                found = [bcs_ref[j, 0, n] for n in range(NZB)]
                 for t in range(NCS):
                     where = jnp.int32(NB)
                     for n in range(NZB):
                         where = jnp.where(found[n] == targets[t], j * NZB + n, where)
-                    rhs[m * BLK:(m + 1) * BLK, t * BLK:(t + 1) * BLK] = blocks[where]
-            acc = jnp.dot(lhs[...], rhs[...], preferred_element_type=jnp.float32)
-            if s == 0:
+                    rhs[m * BLK:(m + 1) * BLK, t * BLK:(t + 1) * BLK] = b_own[where]
+            part[i] = jnp.dot(lhs[...], rhs[...], preferred_element_type=jnp.float32)
+
+    def multiply_pair(p):
+        k_panel = lax.rem(me_r + 1, n_row)
+        place = owner_ref[me_r, k_panel]
+        holder = place // 2
+        slot = lax.rem(place, 2)
+
+        @pl.loop(0, KB)
+        def _(i):
+            targets = [cc_ref[i, 0, t] for t in range(NCS)]
+            stored = [acs[holder, m, slot, i] for m in range(NZA)]
+            for e in range(2):
+                j = 2 * p + e
+                width = size_ref[k_panel * KB + j]
+                block = None
+                for m in range(NZA):
+                    flag = (stored[m] == j).astype(jnp.float32).astype(jnp.bfloat16)
+                    one = full1[pl.ds(pl.multiple_of((i * NZA + m) * BLK, BLK), BLK), :] * flag
+                    block = one if block is None else block + one
+                lhs2[:, e * BLK:(e + 1) * BLK] = jnp.where(lane < width, block, jnp.zeros((), jnp.bfloat16))
+                found = [bns[j, 0, n] for n in range(NZB)]
+                for t in range(NCS):
+                    where = jnp.int32(NPB)
+                    for n in range(NZB):
+                        where = jnp.where(found[n] == targets[t], e * NZB + n, where)
+                    rhs2[e * BLK:(e + 1) * BLK, t * BLK:(t + 1) * BLK] = b_next[p][where]
+            acc = part[i] + jnp.dot(lhs2[...], rhs2[...], preferred_element_type=jnp.float32)
+            if p < 2:
                 part[i] = acc
             else:
-                acc = acc + part[i]
                 height = size_ref[me_r * KB + i]
                 for t in range(NCS):
                     wide = size_ref[me_c * CB + targets[t]]
                     inside = (line < height) & (lane < wide)
                     o_ref[i, t] = jnp.where(inside, acc[:, t * BLK:(t + 1) * BLK], 0.0).astype(jnp.bfloat16)
+
+    def have_pair(p):
+        @pl.when(core == 0)
+        def _():
+            for k in range(p * NPB, (p + 1) * NPB):
+                straight[k].wait_recv()
+
+        @pl.when(core == 1)
+        def _():
+            for k in range(p * NPB, (p + 1) * NPB):
+                if k < n_even:
+                    straight[k].wait_recv()
+                else:
+                    rounds[k - n_even][3].wait_recv()
 
     def indices():
         own_ac.wait()
@@ -338,25 +378,29 @@
     first(0)
     first(1)
     steps = NCHUNK + 5
-    more_b(B_FIRST)
-    leg(LEGS)
-    per = -(-(n_even - B_FIRST) // (steps - 1))
+    more_b(FRONT)
+    leg(L_FRONT)
     for c in range(steps):
         for lag, act in ((5, pass_on), (4, chain_c), (3, chain_b), (2, chain_a), (1, gather_slice), (0, relay)):
             if 0 <= c - lag < NCHUNK:
                 act(c - lag)
         if c + 2 < NCHUNK:
             first(c + 2)
-        more_b(per)
-        leg(LEGS)
-        if c == steps - 6:
+        more_b(MID if c < NCHUNK + 5 else NB)
+        leg(L_MID if c < NCHUNK + 5 else L_LATE)
+        if c == steps - 4:
             indices()
     more_b(NB)
+    more_b(NB)
     landed(0)
-    leg(LEGS * 2)
-    multiply(0, 0, KB)
+    leg(L_LATE)
+    multiply_first()
     leg(len(legs))
     landed(1)
+    have_pair(0)
+    multiply_pair(0)
+    have_pair(1)
+    multiply_pair(1)
     for c in range(NCHUNK):
         for cp in y1s[c]:
             cp.wait_send()
@@ -377,21 +421,17 @@
             cp.wait_send()
         for cps in rounds:
             cps[0].wait_send()
-        for cp in straight:
-            cp.wait_recv()
 
     @pl.when(core == 1)
     def _():
-        for cp in straight[:n_even]:
-            cp.wait_recv()
         for cps in rounds:
-            cps[3].wait_recv()
             for cp in cps[1:]:
                 cp.wait_send()
         for cp in straight:
             cp.wait_send()
 
-    multiply(1, 0, KB)
+    have_pair(2)
+    multiply_pair(2)
 
 
 def local(n_row, n_col, a_vals, a_cols, b_vals, b_cols, c_cols, panel_owner, atom_size):
@@ -428,19 +468,23 @@
             pltpu.VMEM((NCHUNK, CH, BLK), bf),
             pltpu.VMEM((ROWS, BLK), bf),
             pltpu.VMEM((ROWS, BLK), bf),
-            pltpu.VMEM((3, NRG, RB // NRG, BLK, BLK), bf),
+            pltpu.VMEM((3, RB, BLK, BLK), bf),
             pltpu.VMEM((NB + 1, BLK, BLK), bf),
-            pltpu.VMEM((NB + 1, BLK, BLK), bf),
+            pltpu.VMEM((NPB + 1, BLK, BLK), bf),
+            pltpu.VMEM((NPB + 1, BLK, BLK), bf),
+            pltpu.VMEM((NPB + 1, BLK, BLK), bf),
             pltpu.VMEM((KB, BLK, NCS * BLK), jnp.float32),
             pltpu.VMEM((BLK, NZA * BLK), bf),
             pltpu.VMEM((NZA * BLK, NCS * BLK), bf),
+            pltpu.VMEM((BLK, 2 * BLK), bf),
+            pltpu.VMEM((2 * BLK, NCS * BLK), bf),
             pltpu.SMEM((n_col, NZA, 2, KB), jnp.int32),
             pltpu.SMEM((KB, 1, NZB), jnp.int32),
             dma((NCHUNK, 4)), dma((NCHUNK, 4)),
             dma((NCHUNK, 2)), dma((NCHUNK, 2)),
             dma((NCHUNK, 4)), dma((NCHUNK, 4)),
-            dma((NB // PIECE,)), dma((NB // PIECE,)),
-            dma((NRG, 4)), dma((NRG, 4)),
+            dma((NB,)), dma((NB,)),
+            dma((RB, 4)), dma((RB, 4)),
             dma((n_col,)), dma((n_col,)),
             dma((5,)),
         ],

time: 108 us -> 102 us (0.944)
  the two profiles are of different devices: /device:TPU:13 before, /device:TPU:24 now
where the time goes in v3:
time: 102 us
  Pallas kernels  99.2 us (97%)
  local copies, waits for them, and re-layouts  2.41 us (2%)
    pallas_call x1, Pallas kernels, local(): pl.pallas_call(functools.partial(fox_kernel, n_row, n_col), out_shape=(ja...  99.2 us
    unnamed x1, local copies, waits for them, and re-layouts  2.41 us

profile of v3, /device:TPU:24, one launch (start us, length us, event | category | flops | bytes accessed | tf_op | source)
XLA Modules:
  0.0 101.7 jit_solution(15672161136766500645)
XLA Ops:
  0.0 99.2 %fox.1 = (bf16[6,6,128,128]{3,2,1,0:T(8,128)(2,1)}, s32[16,5,2,6]{3,2,1,0:T(2,128)}, s32[6,1,8]{2,1,0:T(1,128)}) custom-call(s32[32,32]{1,0:T(8,128)} %owner_ref.1, s32[192]{0:T(256)} %size_ref.1, s32[6,1,8]{2,1,0:T(1,128)} %bitcast.11, s32[6,1,6]{2,1,0:T(1,128)} %bitcast.14, bf16[2,3840,128]{2,1,0:T(8,128)(2,1)} %bitcast.8, s32[5,2,6]{2,1,0:T(2,128)} %bitcast.13, ...), custom_call_target="tpu_custom_call" | custom-call | tf_op jit(solution)/shard_map/fox/pallas_call | solution.py:448
  99.2 2.4 %copy.9 = bf16[1,1,6,6,128,128]{5,4,3,2,1,0:T(8,128)(2,1)} copy(bf16[1,1,6,6,128,128]{5,4,3,2,1,0:T(8,128)(2,1)} %bitcast.10) | data formatting | bytes 2359296

commit v4 on v3

--- a/solution.py
+++ b/solution.py
@@ -384,9 +384,10 @@
         for lag, act in ((5, pass_on), (4, chain_c), (3, chain_b), (2, chain_a), (1, gather_slice), (0, relay)):
             if 0 <= c - lag < NCHUNK:
                 act(c - lag)
+            if lag in (4, 2, 0):
+                more_b(1)
         if c + 2 < NCHUNK:
             first(c + 2)
-        more_b(MID if c < NCHUNK + 5 else NB)
         leg(L_MID if c < NCHUNK + 5 else L_LATE)
         if c == steps - 4:
             indices()

time: 102 us -> 102 us (level)
  the two profiles are of different devices: /device:TPU:24 before, /device:TPU:31 now
where the time goes in v4:
time: 102 us; the launch traced here: 101 us
  Pallas kernels  99 us (97%)
  local copies, waits for them, and re-layouts  2.41 us (2%)
    pallas_call x1, Pallas kernels, local(): pl.pallas_call(functools.partial(fox_kernel, n_row, n_col), out_shape=(ja...  99 us
    unnamed x1, local copies, waits for them, and re-layouts  2.41 us

profile of v4, /device:TPU:31, one launch (start us, length us, event | category | flops | bytes accessed | tf_op | source)
XLA Modules:
  0.0 101.4 jit_solution(13209595312004617259)
XLA Ops:
  0.0 99.0 %fox.1 = (bf16[6,6,128,128]{3,2,1,0:T(8,128)(2,1)}, s32[16,5,2,6]{3,2,1,0:T(2,128)}, s32[6,1,8]{2,1,0:T(1,128)}) custom-call(s32[32,32]{1,0:T(8,128)} %owner_ref.1, s32[192]{0:T(256)} %size_ref.1, s32[6,1,8]{2,1,0:T(1,128)} %bitcast.11, s32[6,1,6]{2,1,0:T(1,128)} %bitcast.14, bf16[2,3840,128]{2,1,0:T(8,128)(2,1)} %bitcast.8, s32[5,2,6]{2,1,0:T(2,128)} %bitcast.13, ...), custom_call_target="tpu_custom_call" | custom-call | tf_op jit(solution)/shard_map/fox/pallas_call | solution.py:449
  99.0 2.4 %copy.9 = bf16[1,1,6,6,128,128]{5,4,3,2,1,0:T(8,128)(2,1)} copy(bf16[1,1,6,6,128,128]{5,4,3,2,1,0:T(8,128)(2,1)} %bitcast.10) | data formatting | bytes 2359296
